TPU v7x, 256 devices: a whole 4x4x8 slice. The times are simulated.
256 devices in a mesh: det: 64 (over x, z, core), head: 4 (over y).
Axes of the slice: x: 4, y: 4, z: 8, core: 2. Of those that a mesh axis runs over, the one named last changes fastest.
Arguments:
- elements: bfloat16 [32768, 1024], P('det'), may hold values from -6 to 6
- element_types: int32 [32768], P('det'), may hold values from 0 to 1, as said below
- handover_counts: int32 [64, 64], replicated, may hold values from 0 to 16, as said below
- block_lists: int32 [256, 16], P('det'), may hold values from 0 to 255, as said below
- w_first: bfloat16 [2, 1024, 2048], P(None, None, 'head'), may hold values from -0.1875 to 0.1875
- w_second: bfloat16 [2, 2048, 1024], P(None, 'head'), may hold values from -0.125 to 0.125
- w_query: bfloat16 [1024, 1024], P(None, 'head'), may hold values from -3 to 3
- key_value_weight: bfloat16 [1024, 2, 256], P(None, None, 'head'), may hold values from -0.1875 to 0.1875
- attention_cotangent: bfloat16 [32768, 1024], P('det', 'head'), may hold values from -6 to 6
Outputs:
- attended: bfloat16 [32768, 1024], P('det', 'head')
- x_grad: bfloat16 [32768, 1024], P('det', 'head')
Inputs may be any that keep to these rules, and one draw needn't show every extreme that they name: `element_types`: of the 512 elements of each device of det, exactly 256 are of each type. `handover_counts`: row d, column e counts the elements that device d of det hands to device e; every row and every column sums to 512; some entries equal 16. `block_lists`: key block k is held by device k // 4 of det; the 16 entries of a query block may repeat; the lists of the 4 query blocks of one device together name exactly 1 block, counted with repeats, held by each device of det.
All inputs are finite; a program needn't handle non-finite values.
Results may differ from a plain program's by a relative error of at most 0.024.
The roundings to bfloat16 on the way count: a program that leaves them out, or rounds other values in their place, can miss the bound.
Values may be sent and summed in bfloat16 or wider, within the bound.
A program may use at most 64 MiB of HBM per device.

v0:
```python
import jax
import jax.numpy as jnp
from jax import lax
from jax.sharding import PartitionSpec as P

HEAD_SIZE = 64
BLOCK_ROWS = 128
LISTED_COUNT = 16
GROUP_HEADS = 4


def exclusive(counts, reduce_axis):
    return jnp.cumsum(counts, axis=reduce_axis, dtype=jnp.int32) - counts


def pack_rows(source_rows, starts, amounts, capacity):
    slot_ids = jnp.arange(capacity, dtype=jnp.int32)
    row_index = jnp.clip(starts[:, None] + slot_ids[None, :], 0, source_rows.shape[0] - 1)
    usable = slot_ids[None, :] < amounts[:, None]
    picked = source_rows[row_index.reshape(-1)].reshape(
        amounts.shape[0], capacity, source_rows.shape[1]
    )
    return jnp.where(usable[:, :, None], picked, jnp.zeros_like(picked))


def unpack_rows(received, starts, amounts, total_rows):
    peer_count, capacity = (received.shape[0], received.shape[1])
    within = jnp.arange(total_rows, dtype=jnp.int32)
    end_rows = starts + amounts
    peer_ids = jnp.sum(
        (end_rows[None, :] <= within[:, None]).astype(jnp.int32), axis=1, dtype=jnp.int32
    )
    slot_ids = within - starts[peer_ids]
    flattened = received.reshape(peer_count * capacity, received.shape[2])
    return flattened[peer_ids * capacity + slot_ids]


def attend(query_block_one, cotangent_block, key_block_rows, value_block_rows):
    score_scaling = HEAD_SIZE ** (-0.5)
    score_matrix = (
        jnp.einsum(
            "oenl,iel->enoi", query_block_one, key_block_rows, preferred_element_type=jnp.float32
        )
        * score_scaling
    )
    row_max = jnp.max(score_matrix, axis=-1, keepdims=True)
    exp_scores = jnp.exp(score_matrix - row_max)
    probability = exp_scores / jnp.sum(exp_scores, axis=-1, keepdims=True)
    probability_bfloat = probability.astype(jnp.bfloat16)
    attended = jnp.einsum(
        "vnys,svx->yvnx", probability_bfloat, value_block_rows, preferred_element_type=jnp.float32
    ).astype(jnp.bfloat16)
    probability_gradient = jnp.einsum(
        "oenl,iel->enoi", cotangent_block, value_block_rows, preferred_element_type=jnp.float32
    )
    row_delta = jnp.sum(probability * probability_gradient, axis=-1, keepdims=True)
    score_gradient = (probability * (probability_gradient - row_delta)).astype(jnp.bfloat16)
    query_gradient = (
        jnp.einsum(
            "vnys,svx->yvnx", score_gradient, key_block_rows, preferred_element_type=jnp.float32
        )
        * score_scaling
    ).astype(jnp.bfloat16)
    key_gradient = (
        jnp.einsum(
            "njtw,tnjs->wns", score_gradient, query_block_one, preferred_element_type=jnp.float32
        )
        * score_scaling
    )
    value_gradient = jnp.einsum(
        "njtw,tnjs->wns", probability_bfloat, cotangent_block, preferred_element_type=jnp.float32
    )
    return (attended, query_gradient, key_gradient, value_gradient)


def shards(
    elements,
    element_types,
    handover_counts,
    block_lists,
    w_first,
    w_second,
    w_query,
    key_value_weight,
    attention_cotangent,
):
    peer_count = lax.axis_size("det")
    my_index = lax.axis_index("det")
    row_count = elements.shape[0]
    model_width = elements.shape[1]
    capacity = 2 * row_count // peer_count
    starts = exclusive(handover_counts, 1)
    offsets = exclusive(handover_counts, 0)
    send_starts = lax.dynamic_index_in_dim(starts, my_index, 0, keepdims=False)
    send_counts = lax.dynamic_index_in_dim(handover_counts, my_index, 0, keepdims=False)
    recv_starts = lax.dynamic_index_in_dim(offsets, my_index, 1, keepdims=False)
    recv_counts = lax.dynamic_index_in_dim(handover_counts, my_index, 1, keepdims=False)
    type_count = w_first.shape[0]
    per_type = row_count // type_count
    type_order = jnp.argsort(element_types, stable=True)
    back_order = (
        jnp.zeros_like(type_order).at[type_order].set(jnp.arange(row_count, dtype=jnp.int32))
    )
    sorted_rows = elements[type_order].reshape(type_count, per_type, model_width)
    preact = jnp.einsum("trd,tdh->trh", sorted_rows, w_first, preferred_element_type=jnp.float32)
    hidden = jax.nn.gelu(preact).astype(jnp.bfloat16)
    sorted_mlp = jnp.einsum("trh,thd->trd", hidden, w_second, preferred_element_type=jnp.float32)
    partial_mlp = sorted_mlp.reshape(row_count, model_width)[back_order]
    mlp_sum = lax.psum(partial_mlp, "head")
    mixed = (elements.astype(jnp.float32) + mlp_sum).astype(jnp.bfloat16)
    outbound = pack_rows(mixed, send_starts, send_counts, capacity)
    inbound = lax.all_to_all(outbound, "det", split_axis=0, concat_axis=0, tiled=True)
    moved = unpack_rows(inbound, recv_starts, recv_counts, row_count)
    kv_width = key_value_weight.shape[2]
    key_value_flat = key_value_weight.reshape(model_width, 2 * kv_width)
    query_rows_all = jnp.dot(moved, w_query, preferred_element_type=jnp.float32).astype(
        jnp.bfloat16
    )
    key_value_pairs = jnp.dot(moved, key_value_flat, preferred_element_type=jnp.float32).astype(
        jnp.bfloat16
    )
    blocks_dev = row_count // BLOCK_ROWS
    slot_count = blocks_dev * LISTED_COUNT
    per_pair = slot_count // peer_count
    flat_list = block_lists.reshape(slot_count)
    owners = flat_list // blocks_dev
    local_ids = flat_list % blocks_dev
    slot_order = jnp.arange(slot_count, dtype=jnp.int32)
    earlier = (owners[:, None] == owners[None, :]) & (slot_order[None, :] < slot_order[:, None])
    slot_rank = jnp.sum(earlier.astype(jnp.int32), axis=1, dtype=jnp.int32)
    position = owners * per_pair + slot_rank
    requests = (
        jnp.zeros((slot_count,), jnp.int32)
        .at[position]
        .set(local_ids)
        .reshape(peer_count, per_pair)
    )
    wanted = lax.all_to_all(requests, "det", split_axis=0, concat_axis=0, tiled=True)
    all_keys = lax.all_gather(key_value_pairs, "det", axis=0, tiled=True)
    listed = all_keys.reshape(-1, BLOCK_ROWS, 2 * kv_width)[flat_list]
    listed = listed.reshape(blocks_dev, LISTED_COUNT * BLOCK_ROWS, 2 * kv_width)
    kv_heads = kv_width // HEAD_SIZE
    query_block_list = query_rows_all.reshape(
        blocks_dev, BLOCK_ROWS, kv_heads, GROUP_HEADS, HEAD_SIZE
    )
    cotangent_blocks = attention_cotangent.reshape(
        blocks_dev, BLOCK_ROWS, kv_heads, GROUP_HEADS, HEAD_SIZE
    )

    def one_block(inputs):
        query_block_one, cotangent_block, key_value_rows = inputs
        key_block_rows = key_value_rows[:, :kv_width].reshape(
            LISTED_COUNT * BLOCK_ROWS, kv_heads, HEAD_SIZE
        )
        value_block_rows = key_value_rows[:, kv_width:].reshape(
            LISTED_COUNT * BLOCK_ROWS, kv_heads, HEAD_SIZE
        )
        return attend(query_block_one, cotangent_block, key_block_rows, value_block_rows)

    attended, query_gradient, key_gradient, value_gradient = lax.map(
        one_block, (query_block_list, cotangent_blocks, listed)
    )
    slot_gradients = jnp.concatenate(
        [
            key_gradient.reshape(blocks_dev, LISTED_COUNT * BLOCK_ROWS, kv_width),
            value_gradient.reshape(blocks_dev, LISTED_COUNT * BLOCK_ROWS, kv_width),
        ],
        axis=2,
    )
    slot_gradients = slot_gradients.reshape(slot_count, BLOCK_ROWS, 2 * kv_width).astype(
        jnp.bfloat16
    )
    returned = (
        jnp.zeros_like(slot_gradients)
        .at[position]
        .set(slot_gradients)
        .reshape(peer_count, per_pair, BLOCK_ROWS, 2 * kv_width)
    )
    collected = lax.all_to_all(returned, "det", split_axis=0, concat_axis=0, tiled=True)
    collected = collected.reshape(slot_count, BLOCK_ROWS, 2 * kv_width).astype(jnp.float32)
    key_gradient_total = (
        jnp.zeros((blocks_dev, BLOCK_ROWS, 2 * kv_width), jnp.float32)
        .at[wanted.reshape(-1)]
        .add(collected)
    )
    key_bfloat = key_gradient_total.reshape(row_count, 2 * kv_width).astype(jnp.bfloat16)
    contract = (((1,), (1,)), ((), ()))
    partial_back = lax.dot_general(
        query_gradient.reshape(row_count, -1), w_query, contract, preferred_element_type=jnp.float32
    )
    partial_back = partial_back + lax.dot_general(
        key_bfloat, key_value_flat, contract, preferred_element_type=jnp.float32
    )
    back_sum = lax.psum(partial_back, "head").astype(jnp.bfloat16)
    outbound_back = pack_rows(back_sum, recv_starts, recv_counts, capacity)
    inbound_back = lax.all_to_all(outbound_back, "det", split_axis=0, concat_axis=0, tiled=True)
    upstream = unpack_rows(inbound_back, send_starts, send_counts, row_count)
    sorted_up = upstream[type_order].reshape(type_count, per_type, model_width)
    hidden_grad = jnp.einsum(
        "trd,thd->trh", sorted_up, w_second, preferred_element_type=jnp.float32
    )
    preact_grad = jax.vjp(jax.nn.gelu, preact)[1](hidden_grad)[0].astype(jnp.bfloat16)
    sorted_input = jnp.einsum(
        "trh,tdh->trd", preact_grad, w_first, preferred_element_type=jnp.float32
    )
    input_part = sorted_input.reshape(row_count, model_width)[back_order]
    input_share = lax.psum_scatter(input_part, "head", scatter_dimension=1, tiled=True)
    share_width = input_share.shape[1]
    own_upstream = lax.dynamic_slice_in_dim(
        upstream, lax.axis_index("head") * share_width, share_width, 1
    )
    x_grad = (own_upstream.astype(jnp.float32) + input_share).astype(jnp.bfloat16)
    return (attended.reshape(row_count, -1), x_grad)


def solution(mesh):
    return jax.shard_map(
        shards,
        mesh=mesh,
        in_specs=(
            P("det", None),
            P("det"),
            P(),
            P("det", None),
            P(None, None, "head"),
            P(None, "head", None),
            P(None, "head"),
            P(None, None, "head"),
            P("det", "head"),
        ),
        out_specs=(P("det", "head"), P("det", "head")),
        check_vma=False,
    )
```

profile of v0, /device:TPU:1, one launch (start us, length us, event | category | flops | bytes accessed | tf_op | source)
XLA Modules:
  0.0 602.9 jit_solution(14626544373594868727)
XLA Ops:
  7.2 4.6 sort.17
  14.3 4.1 gather_fusion
  22.9 5.3 gather_fusion.1
  29.4 66.3 %all-reduce.3.cloned.1.call-done = f32[512,1024]{1,0:T(8,128)} async-done(((f32[512,1024]{1,0:T(8,128)}), f32[512,1024]{1,0:T(8,128)}) %all-reduce.3.cloned.1.call-update) | async-done | bytes 2097168 | tf_op jit(solution)/shard_map/psum | solution.py:109
  98.0 5.4 gather_fusion.2
  103.4 3.2 broadcast_select_fusion.1
  106.6 11.0 %all-to-all-start = ((bf16[64,16,1024]{2,1,0:T(8,128)(2,1)}), bf16[64,16,1024]{2,1,0:T(8,128)(2,1)}, u32[]{:S(2)}, u32[]{:S(2)}) async-start(bf16[64,16,1024]{2,1,0:T(8,128)(2,1)} %broadcast_select_fusion.1), calls=%async_computation | async-start | bytes 4194304 | tf_op jit(solution)/shard_map/all_to_all | solution.py:112
  123.6 4.3 compare_select_fusion.12
  128.2 4.3 compare_select_fusion.6
  132.9 35.3 %select_select_fusion.1 = s32[512]{0:T(512)S(1)} fusion(pred[512]{0:T(512)(128)(4,1)S(1)} %get-tuple-element.224, pred[512]{0:T(512)(128)(4,1)S(1)} %get-tuple-element.223, pred[512]{0:T(512)(128)(4,1)S(1)} %get-tuple-element.222, pred[512]{0:T(512)(128)(4,1)S(1)} %get-tuple-element.221, pred[512]{0:T(512)(128)(4,1)S(1)} %get-tuple-element.220, ...), kind=kLoop, calls=%fused_computation.250 | loop fusion | flops 29184 | bytes 33508 | tf_op jit(solution)/shard_map/gather | solution.py:33
  168.3 35.6 %select_select_fusion = s32[512]{0:T(512)S(1)} fusion(pred[512]{0:T(512)(128)(4,1)S(1)} %get-tuple-element.167, pred[512]{0:T(512)(128)(4,1)S(1)} %get-tuple-element.166, pred[512]{0:T(512)(128)(4,1)S(1)} %get-tuple-element.165, pred[512]{0:T(512)(128)(4,1)S(1)} %get-tuple-element.164, pred[512]{0:T(512)(128)(4,1)S(1)} %get-tuple-element.163, ...), kind=kLoop, calls=%fused_computation.249 | loop fusion | flops 29184 | bytes 33508 | tf_op jit(solution)/shard_map/gather | solution.py:33
  204.0 4.6 gather_fusion.3
  210.1 10.0 %scatter_custom_fusion.1 = s32[64]{0:T(128)S(1)} fusion(s32[64]{0:T(128)S(1)} %get-tuple-element.385, s32[64]{0:T(128)S(1)} %get-tuple-element.383, s32[]{:T(128)} %constant.56.clone.1), kind=kCustom, calls=%fused_computation.271 | custom fusion | bytes 260 | tf_op jit(solution)/shard_map/scatter | solution.py:135
  220.8 10.3 %all-to-all-start.1 = ((s32[64,1,1]{2,1,0:T(1,128)}), s32[64,1,1]{2,1,0:T(1,128)S(1)}, u32[]{:S(2)}, u32[]{:S(2)}) async-start(s32[64,1,1]{2,1,0:T(1,128)} %copy.91), calls=%async_computation.1 | async-start | bytes 65536 | tf_op jit(solution)/shard_map/all_to_all | solution.py:138
  237.2 55.5 %all-gather.2.cloned.1.call-done = bf16[32768,128]{1,0:T(8,128)(2,1)} async-done(((bf16[512,128]{1,0:T(8,128)(2,1)}), bf16[32768,128]{1,0:T(8,128)(2,1)}) %all-gather.2.cloned.1.call-update) | async-done | bytes 8388624 | tf_op jit(solution)/shard_map/all_gather | solution.py:139
  292.7 5.6 gather_fusion.4
  298.3 41.0 %while.16 = (s32[]{:T(128)}, bf16[4,128,1,4,64]{1,4,3,2,0:T(8,128)(2,1)}, bf16[4,128,1,4,64]{1,4,3,2,0:T(8,128)(2,1)}, bf16[4,2048,1,64]{1,3,2,0:T(8,128)(2,1)},...) while((s32[]{:T(128)}, ...), condition=%wide.region_10.11_spmd, body=%wide.region_6.10_spmd.sunk | while | flops 830700032 | bytes 62289140 | solution.py:160
  349.5 4.2 copy.94
  355.6 10.0 %scatter_fusion = bf16[64,128,128]{2,1,0:T(8,128)(2,1)} fusion(bf16[64,128,128]{2,1,0:T(8,128)(2,1)} %broadcast_in_dim.43, s32[64]{0:T(128)S(1)} %get-tuple-element.385, bf16[64,128,128]{2,1,0:T(8,128)(2,1)} %copy.94), kind=kCustom, calls=%fused_computation.11 | custom fusion | bytes 6291712 | tf_op jit(solution)/shard_map/scatter | solution.py:176
  365.6 6.0 %all-to-all-start.2 = ((bf16[64,1,128,128]{3,2,1,0:T(8,128)(2,1)}), bf16[64,1,128,128]{3,2,1,0:T(8,128)(2,1)}, u32[]{:S(2)}, u32[]{:S(2)}) async-start(bf16[64,1,128,128]{3,2,1,0:T(8,128)(2,1)} %bitcast.379), calls=%async_computation.2 | async-start | bytes 4194304 | tf_op jit(solution)/shard_map/all_to_all | solution.py:179
  373.3 49.4 %all-to-all-done.2 = bf16[64,1,128,128]{3,2,1,0:T(8,128)(2,1)} async-done(((bf16[64,1,128,128]{3,2,1,0:T(8,128)(2,1)}), bf16[64,1,128,128]{3,2,1,0:T(8,128)(2,1)}, u32[]{:S(2)}, u32[]{:S(2)}) %all-to-all-start.2) | async-done | bytes 2097184 | tf_op jit(solution)/shard_map/all_to_all | solution.py:179
  422.7 4.0 bitcast_convert_fusion
  426.8 8.8 %scatter_fusion.1 = f32[4,128,128]{2,1,0:T(8,128)S(1)} fusion(f32[4,128,128]{2,1,0:T(8,128)S(1)} %broadcast_in_dim.42, s32[64]{0:T(128)S(1)} %fusion.73, f32[64,128,128]{2,1,0:T(8,128)} %bitcast_convert_fusion), kind=kCustom, calls=%fused_computation.12 | custom fusion | flops 1048576 | bytes 12583168 | tf_op jit(solution)/shard_map/scatter-add | solution.py:184
  438.5 42.7 %all-reduce.4 = bf16[512,1024]{1,0:T(8,128)(2,1)S(1)} all-reduce(f32[512,1024]{1,0:T(8,128)} %convolution_add_fusion), channel_id=1, replica_groups=mesh['det'=64,'head'=4] {'head'}, use_global_device_ids=true, to_apply=%region_15.16 | all-reduce | flops 524288 | bytes 3145728 | tf_op jit(solution)/shard_map/psum | solution.py:194
  481.2 5.4 gather_fusion.5
  486.6 3.2 broadcast_select_fusion
  489.8 8.1 %all-to-all-start.3 = ((bf16[64,16,1024]{2,1,0:T(8,128)(2,1)}), bf16[64,16,1024]{2,1,0:T(8,128)(2,1)}, u32[]{:S(2)}, u32[]{:S(2)}) async-start(bf16[64,16,1024]{2,1,0:T(8,128)(2,1)} %broadcast_select_fusion), calls=%async_computation.3 | async-start | bytes 4194304 | tf_op jit(solution)/shard_map/all_to_all | solution.py:196
  497.9 51.1 %all-to-all-done.3 = bf16[64,16,1024]{2,1,0:T(8,128)(2,1)} async-done(((bf16[64,16,1024]{2,1,0:T(8,128)(2,1)}), bf16[64,16,1024]{2,1,0:T(8,128)(2,1)}, u32[]{:S(2)}, u32[]{:S(2)}) %all-to-all-start.3) | async-done | bytes 2097184 | tf_op jit(solution)/shard_map/all_to_all | solution.py:196
  548.9 4.6 gather_fusion.6
  556.3 5.3 fusion.53
  561.7 5.2 gather_fusion.8
  571.1 23.1 %reduce-scatter.2.cloned.1.call-done = f32[512,256]{1,0:T(8,128)} async-done(((f32[512,1024]{1,0:T(8,128)}), f32[512,256]{1,0:T(8,128)}) %reduce-scatter.2.cloned.1.call-update) | async-done | bytes 524304 | tf_op jit(solution)/shard_map/reduce_scatter | solution.py:207
  (188 shorter events, 91.5 us)
Async XLA Ops:
  7.2 13.6 %copy-start = (bf16[2,512,1024]{2,1,0:T(8,128)(2,1)S(1)}, bf16[2,512,1024]{2,1,0:T(8,128)(2,1)}, u32[]{:S(2)}) copy-start(bf16[2,512,1024]{2,1,0:T(8,128)(2,1)} %param.16) | copy-start | bytes 6291460
  7.2 88.6 %all-reduce.3.cloned.1.call-start = ((), (), s32[]{:S(2)}) async-start(), calls=%async_computation.5 | async-start | bytes 4194304 | tf_op jit(solution)/shard_map/psum | solution.py:109
  11.8 6.6 %copy-start.13 = (s32[1024]{0:T(1024)}, s32[1024]{0:T(1024)S(1)}, u32[]{:S(2)}) copy-start(s32[1024]{0:T(1024)S(1)} %pad_clamp_fusion.4) | copy-start | bytes 12292
  14.3 8.6 %copy-start.15 = (s32[1024]{0:T(1024)}, s32[1024]{0:T(1024)S(1)}, u32[]{:S(2)}) copy-start(s32[1024]{0:T(1024)S(1)} %pad_clamp_fusion.3) | copy-start | bytes 12292
  20.7 2.2 copy-start.1
  106.6 97.4 %all-to-all-start = ((bf16[64,16,1024]{2,1,0:T(8,128)(2,1)}), bf16[64,16,1024]{2,1,0:T(8,128)(2,1)}, u32[]{:S(2)}, u32[]{:S(2)}) async-start(bf16[64,16,1024]{2,1,0:T(8,128)(2,1)} %broadcast_select_fusion.1), calls=%async_computation | async-start | bytes 4194304 | tf_op jit(solution)/shard_map/all_to_all | solution.py:112
  117.6 175.2 %all-gather.2.cloned.1.call-start = ((), (), s32[]{:S(2)}) async-start(), calls=%async_computation.6 | async-start | bytes 8519680 | tf_op jit(solution)/shard_map/all_gather | solution.py:139
  203.9 4.7 copy-start.6
  204.0 5.8 copy-start.17
  220.8 144.7 %all-to-all-start.1 = ((s32[64,1,1]{2,1,0:T(1,128)}), s32[64,1,1]{2,1,0:T(1,128)S(1)}, u32[]{:S(2)}, u32[]{:S(2)}) async-start(s32[64,1,1]{2,1,0:T(1,128)} %copy.91), calls=%async_computation.1 | async-start | bytes 65536 | tf_op jit(solution)/shard_map/all_to_all | solution.py:138
  300.4 1.2 copy-start.4
  300.4 1.3 copy-start.10
  302.6 1.3 copy-start.5
  303.9 1.2 copy-start.2
  310.6 1.2 copy-start.4
  310.7 1.3 copy-start.10
  312.9 1.3 copy-start.5
  314.2 1.2 copy-start.2
  320.9 1.2 copy-start.4
  320.9 1.3 copy-start.10
  323.1 1.3 copy-start.5
  331.2 1.2 copy-start.4
  331.2 1.3 copy-start.10
  333.4 1.3 copy-start.5
  334.7 1.2 copy-start.2
  365.6 7.6 %copy-start.12 = (bf16[4,128,1,4,64]{1,4,3,2,0:T(8,128)(2,1)S(1)}, bf16[4,128,1,4,64]{1,4,3,2,0:T(8,128)(2,1)}, u32[]{:S(2)}) copy-start(bf16[4,128,1,4,64]{1,4,3,2,0:T(8,128)(2,1)} %get-tuple-element.50) | copy-start | bytes 786436
  365.6 57.2 %all-to-all-start.2 = ((bf16[64,1,128,128]{3,2,1,0:T(8,128)(2,1)}), bf16[64,1,128,128]{3,2,1,0:T(8,128)(2,1)}, u32[]{:S(2)}, u32[]{:S(2)}) async-start(bf16[64,1,128,128]{3,2,1,0:T(8,128)(2,1)} %bitcast.379), calls=%async_computation.2 | async-start | bytes 4194304 | tf_op jit(solution)/shard_map/all_to_all | solution.py:179
  426.8 8.8 %copy-start.7 = (bf16[1024,2,64]{0,2,1:T(8,128)(2,1)S(1)}, bf16[1024,2,64]{0,2,1:T(8,128)(2,1)}, u32[]{:S(2)}) copy-start(bf16[1024,2,64]{0,2,1:T(8,128)(2,1)} %param.18) | copy-start | bytes 786436
  489.8 59.2 %all-to-all-start.3 = ((bf16[64,16,1024]{2,1,0:T(8,128)(2,1)}), bf16[64,16,1024]{2,1,0:T(8,128)(2,1)}, u32[]{:S(2)}, u32[]{:S(2)}) async-start(bf16[64,16,1024]{2,1,0:T(8,128)(2,1)} %broadcast_select_fusion), calls=%async_computation.3 | async-start | bytes 4194304 | tf_op jit(solution)/shard_map/all_to_all | solution.py:196
  497.8 96.4 %reduce-scatter.2.cloned.1.call-start = ((), (), s32[]{:S(2)}) async-start(), calls=%async_computation.7 | async-start | bytes 2621440 | tf_op jit(solution)/shard_map/reduce_scatter | solution.py:207
  548.9 4.6 copy-start.14
  556.3 5.3 copy-start.16
  (8 other events, 8.5 us)
Sparse Core Ops, SparseCore 0:
  28.3 67.4 all-reduce.2
  209.9 82.8 all-gather.1
  567.0 27.1 reduce-scatter.1
where the time goes:
time: 614 us; the launch traced here: 603 us
  waiting for transfers between devices  245 us (40%)
  other arithmetic  121 us (20%)
  local copies, waits for them, and re-layouts  103 us (17%)
  blocking collectives  42.7 us (7%)
  matrix products  40.3 us (7%)
  starting transfers between devices  35.6 us (6%)
  between operations  14.6 us (2%)
    gather x6, other arithmetic, unpack_rows(): slot_ids = within - starts[peer_ids]  80.3 us
    psum x1, waiting for transfers between devices, shards(): mlp_sum = lax.psum(partial_mlp, 'head')  66.3 us
    all_gather x1, waiting for transfers between devices, shards(): all_keys = lax.all_gather(key_value_pairs, 'det', axis=0, tiled=True)  55.5 us
    all_to_all x1, waiting for transfers between devices, shards(): lax.all_to_all(outbound_back, 'det', split_axis=0, concat_axis=0, tiled=T...  51.1 us
    all_to_all x1, waiting for transfers between devices, shards(): lax.all_to_all(returned, 'det', split_axis=0, concat_axis=0, tiled=True)  49.4 us
    psum x1, blocking collectives, shards(): back_sum = lax.psum(partial_back, 'head').astype(jnp.bfloat16)  42.7 us
    reduce_scatter x1, waiting for transfers between devices, shards(): lax.psum_scatter(input_part, 'head', scatter_dimension=1, tiled=True)  23.1 us
  transfers between devices with their start and end apart: 7, of which 5 were waited for; matrix products, arithmetic and copies ran while one was open for 30% of the time, Pallas kernels for 0%

commit v1 on v0

--- a/solution.py
+++ b/solution.py
@@ -7,6 +7,12 @@
 BLOCK_ROWS = 128
 LISTED_COUNT = 16
 GROUP_HEADS = 4
+
+
+def _draw_sectors(q_in):
+    z2 = jnp.stack([q_in for _ in range(lax.axis_size("det"))], axis=0)
+    ready = jnp.concatenate(lax.all_to_all(z2, "det", 0, 0), axis=0)
+    return ready
 
 
 def exclusive(counts, reduce_axis):
@@ -136,7 +142,7 @@
         .reshape(peer_count, per_pair)
     )
     wanted = lax.all_to_all(requests, "det", split_axis=0, concat_axis=0, tiled=True)
-    all_keys = lax.all_gather(key_value_pairs, "det", axis=0, tiled=True)
+    all_keys = _draw_sectors(key_value_pairs)
     listed = all_keys.reshape(-1, BLOCK_ROWS, 2 * kv_width)[flat_list]
     listed = listed.reshape(blocks_dev, LISTED_COUNT * BLOCK_ROWS, 2 * kv_width)
     kv_heads = kv_width // HEAD_SIZE

time: 614 us -> 741 us (1.21)
  waiting for transfers between devices: 245 us -> 370 us
  starting transfers between devices: 35.6 us -> 47.7 us
    all_to_all x0 -> x1, waiting for transfers between devices: none -> 179 us  [_draw_sectors(): ready = jnp.concatenate(lax.all_to_all(z2, 'det', 0, 0), axis=0)]
    all_gather x1 -> x0, waiting for transfers between devices: 55.5 us -> none  [shards(): all_keys = lax.all_gather(key_value_pairs, 'det', axis=0, tiled=True)]
    all_to_all x0 -> x1, starting transfers between devices: none -> 10.6 us  [_draw_sectors(): ready = jnp.concatenate(lax.all_to_all(z2, 'det', 0, 0), axis=0)]
    scatter x1, local copies, waits for them, and re-layouts: 10 us -> 0.77 us  [shards(): requests = jnp.zeros((slot_count,), jnp.int32).at[position].set(local_ids...]
  transfers between devices with their start and end apart: 7 -> 7, of which waited for: 5 -> 5; matrix products, arithmetic and copies ran while one was open for 30% -> 23% of each run, Pallas kernels for 0% -> 0%
where the time goes in v1:
time: 741 us; the launch traced here: 733 us
  waiting for transfers between devices  370 us (50%)
  other arithmetic  122 us (16%)
  local copies, waits for them, and re-layouts  98 us (13%)
  starting transfers between devices  47.7 us (6%)
  blocking collectives  40.7 us (5%)
  matrix products  39.7 us (5%)
  between operations  14.8 us (2%)
    all_to_all x1, waiting for transfers between devices, _draw_sectors(): ready = jnp.concatenate(lax.all_to_all(z2, 'det', 0, 0), axis=0)  179 us
    gather x6, other arithmetic, unpack_rows(): slot_ids = within - starts[peer_ids]  80.9 us
    psum x1, waiting for transfers between devices, shards(): mlp_sum = lax.psum(partial_mlp, 'head')  66.3 us
    all_to_all x1, waiting for transfers between devices, shards(): lax.all_to_all(outbound_back, 'det', split_axis=0, concat_axis=0, tiled=T...  51 us
    all_to_all x1, waiting for transfers between devices, shards(): lax.all_to_all(returned, 'det', split_axis=0, concat_axis=0, tiled=True)  49.3 us
    psum x1, blocking collectives, shards(): back_sum = lax.psum(partial_back, 'head').astype(jnp.bfloat16)  40.7 us
    reduce_scatter x1, waiting for transfers between devices, shards(): lax.psum_scatter(input_part, 'head', scatter_dimension=1, tiled=True)  24.1 us
  transfers between devices with their start and end apart: 7, of which 5 were waited for; matrix products, arithmetic and copies ran while one was open for 23% of the time, Pallas kernels for 0%

profile of v1, /device:TPU:1, one launch (start us, length us, event | category | flops | bytes accessed | tf_op | source)
XLA Modules:
  0.0 732.8 jit_solution(1447657452326822961)
XLA Ops:
  7.2 4.6 sort.17
  14.3 4.1 gather_fusion
  22.9 5.3 gather_fusion.1
  29.5 66.3 %all-reduce.3.cloned.1.call-done = f32[512,1024]{1,0:T(8,128)} async-done(((f32[512,1024]{1,0:T(8,128)}), f32[512,1024]{1,0:T(8,128)}) %all-reduce.3.cloned.1.call-update) | async-done | bytes 2097168 | tf_op jit(solution)/shard_map/psum | solution.py:115
  98.0 5.4 gather_fusion.2
  103.4 3.2 broadcast_select_fusion.1
  106.6 11.7 %all-to-all-start = ((bf16[64,16,1024]{2,1,0:T(8,128)(2,1)}), bf16[64,16,1024]{2,1,0:T(8,128)(2,1)}, u32[]{:S(2)}, u32[]{:S(2)}) async-start(bf16[64,16,1024]{2,1,0:T(8,128)(2,1)} %broadcast_select_fusion.1), calls=%async_computation | async-start | bytes 4194304 | tf_op jit(solution)/shard_map/all_to_all | solution.py:118
  124.2 4.3 compare_select_fusion.12
  128.9 4.4 compare_select_fusion.6
  133.6 35.7 %select_select_fusion.1 = s32[512]{0:T(512)S(1)} fusion(pred[512]{0:T(512)(128)(4,1)S(1)} %get-tuple-element.224, pred[512]{0:T(512)(128)(4,1)S(1)} %get-tuple-element.223, pred[512]{0:T(512)(128)(4,1)S(1)} %get-tuple-element.222, pred[512]{0:T(512)(128)(4,1)S(1)} %get-tuple-element.221, pred[512]{0:T(512)(128)(4,1)S(1)} %get-tuple-element.220, ...), kind=kLoop, calls=%fused_computation.250 | loop fusion | flops 29184 | bytes 33508 | tf_op jit(solution)/shard_map/gather | solution.py:39
  169.4 35.7 %select_select_fusion = s32[512]{0:T(512)S(1)} fusion(pred[512]{0:T(512)(128)(4,1)S(1)} %get-tuple-element.167, pred[512]{0:T(512)(128)(4,1)S(1)} %get-tuple-element.166, pred[512]{0:T(512)(128)(4,1)S(1)} %get-tuple-element.165, pred[512]{0:T(512)(128)(4,1)S(1)} %get-tuple-element.164, pred[512]{0:T(512)(128)(4,1)S(1)} %get-tuple-element.163, ...), kind=kLoop, calls=%fused_computation.249 | loop fusion | flops 29184 | bytes 33508 | tf_op jit(solution)/shard_map/gather | solution.py:39
  205.7 4.6 gather_fusion.3
  210.8 5.2 stack.2
  216.1 10.6 %all-to-all-start.1 = ((bf16[64,512,128]{2,1,0:T(8,128)(2,1)}), bf16[64,512,128]{2,1,0:T(8,128)(2,1)}, u32[]{:S(2)}, u32[]{:S(2)}) async-start(bf16[64,512,128]{2,1,0:T(8,128)(2,1)} %stack.2), calls=%async_computation.1 | async-start | bytes 16777216 | tf_op jit(solution)/shard_map/all_to_all | solution.py:14
  233.6 178.9 %all-to-all-done.1 = bf16[64,512,128]{2,1,0:T(8,128)(2,1)} async-done(((bf16[64,512,128]{2,1,0:T(8,128)(2,1)}), bf16[64,512,128]{2,1,0:T(8,128)(2,1)}, u32[]{:S(2)}, u32[]{:S(2)}) %all-to-all-start.1) | async-done | bytes 8388640 | tf_op jit(solution)/shard_map/all_to_all | solution.py:14
  412.4 6.1 all-to-all-start.2
  418.5 5.6 gather_fusion.4
  424.1 41.0 %while.16 = (s32[]{:T(128)}, bf16[4,128,1,4,64]{1,4,3,2,0:T(8,128)(2,1)}, bf16[4,128,1,4,64]{1,4,3,2,0:T(8,128)(2,1)}, bf16[4,2048,1,64]{1,3,2,0:T(8,128)(2,1)},...) while((s32[]{:T(128)}, ...), condition=%wide.region_10.11_spmd, body=%wide.region_6.10_spmd.sunk | while | flops 830700032 | bytes 62289140 | solution.py:166
  475.3 4.2 copy.94
  481.4 10.0 %scatter_fusion = bf16[64,128,128]{2,1,0:T(8,128)(2,1)} fusion(bf16[64,128,128]{2,1,0:T(8,128)(2,1)} %broadcast_in_dim.43, s32[64]{0:T(128)S(1)} %get-tuple-element.385, bf16[64,128,128]{2,1,0:T(8,128)(2,1)} %copy.94), kind=kCustom, calls=%fused_computation.11 | custom fusion | bytes 6291712 | tf_op jit(solution)/shard_map/scatter | solution.py:182
  491.4 11.0 %all-to-all-start.3 = ((bf16[64,1,128,128]{3,2,1,0:T(8,128)(2,1)}), bf16[64,1,128,128]{3,2,1,0:T(8,128)(2,1)}, u32[]{:S(2)}, u32[]{:S(2)}) async-start(bf16[64,1,128,128]{3,2,1,0:T(8,128)(2,1)} %bitcast.379), calls=%async_computation.3 | async-start | bytes 4194304 | tf_op jit(solution)/shard_map/all_to_all | solution.py:185
  504.1 49.3 %all-to-all-done.3 = bf16[64,1,128,128]{3,2,1,0:T(8,128)(2,1)} async-done(((bf16[64,1,128,128]{3,2,1,0:T(8,128)(2,1)}), bf16[64,1,128,128]{3,2,1,0:T(8,128)(2,1)}, u32[]{:S(2)}, u32[]{:S(2)}) %all-to-all-start.3) | async-done | bytes 2097184 | tf_op jit(solution)/shard_map/all_to_all | solution.py:185
  553.3 4.0 bitcast_convert_fusion
  557.4 8.8 %scatter_fusion.1 = f32[4,128,128]{2,1,0:T(8,128)S(1)} fusion(f32[4,128,128]{2,1,0:T(8,128)S(1)} %broadcast_in_dim.42, s32[64]{0:T(128)S(1)} %fusion.73, f32[64,128,128]{2,1,0:T(8,128)} %bitcast_convert_fusion), kind=kCustom, calls=%fused_computation.12 | custom fusion | flops 1048576 | bytes 12583168 | tf_op jit(solution)/shard_map/scatter-add | solution.py:190
  569.1 40.7 %all-reduce.4 = bf16[512,1024]{1,0:T(8,128)(2,1)S(1)} all-reduce(f32[512,1024]{1,0:T(8,128)} %convolution_add_fusion), channel_id=1, replica_groups=mesh['det'=64,'head'=4] {'head'}, use_global_device_ids=true, to_apply=%region_15.16 | all-reduce | flops 524288 | bytes 3145728 | tf_op jit(solution)/shard_map/psum | solution.py:200
  609.8 5.4 gather_fusion.5
  618.3 8.3 %all-to-all-start.4 = ((bf16[64,16,1024]{2,1,0:T(8,128)(2,1)}), bf16[64,16,1024]{2,1,0:T(8,128)(2,1)}, u32[]{:S(2)}, u32[]{:S(2)}) async-start(bf16[64,16,1024]{2,1,0:T(8,128)(2,1)} %broadcast_select_fusion), calls=%async_computation.4 | async-start | bytes 4194304 | tf_op jit(solution)/shard_map/all_to_all | solution.py:202
  626.7 51.0 %all-to-all-done.4 = bf16[64,16,1024]{2,1,0:T(8,128)(2,1)} async-done(((bf16[64,16,1024]{2,1,0:T(8,128)(2,1)}), bf16[64,16,1024]{2,1,0:T(8,128)(2,1)}, u32[]{:S(2)}, u32[]{:S(2)}) %all-to-all-start.4) | async-done | bytes 2097184 | tf_op jit(solution)/shard_map/all_to_all | solution.py:202
  677.7 4.6 gather_fusion.6
  685.1 5.3 fusion.53
  690.4 5.2 gather_fusion.8
  699.8 24.1 %reduce-scatter.2.cloned.1.call-done = f32[512,256]{1,0:T(8,128)} async-done(((f32[512,1024]{1,0:T(8,128)}), f32[512,256]{1,0:T(8,128)}) %reduce-scatter.2.cloned.1.call-update) | async-done | bytes 524304 | tf_op jit(solution)/shard_map/reduce_scatter | solution.py:213
  (192 shorter events, 94.3 us)
Async XLA Ops:
  7.2 13.6 %copy-start = (bf16[2,512,1024]{2,1,0:T(8,128)(2,1)S(1)}, bf16[2,512,1024]{2,1,0:T(8,128)(2,1)}, u32[]{:S(2)}) copy-start(bf16[2,512,1024]{2,1,0:T(8,128)(2,1)} %param.16) | copy-start | bytes 6291460
  7.2 88.6 %all-reduce.3.cloned.1.call-start = ((), (), s32[]{:S(2)}) async-start(), calls=%async_computation.6 | async-start | bytes 4194304 | tf_op jit(solution)/shard_map/psum | solution.py:115
  11.8 6.6 copy-start.14
  14.3 8.6 %copy-start.16 = (s32[1024]{0:T(1024)}, s32[1024]{0:T(1024)S(1)}, u32[]{:S(2)}) copy-start(s32[1024]{0:T(1024)S(1)} %pad_clamp_fusion.3) | copy-start | bytes 12292
  20.7 2.2 copy-start.1
  106.6 99.2 %all-to-all-start = ((bf16[64,16,1024]{2,1,0:T(8,128)(2,1)}), bf16[64,16,1024]{2,1,0:T(8,128)(2,1)}, u32[]{:S(2)}, u32[]{:S(2)}) async-start(bf16[64,16,1024]{2,1,0:T(8,128)(2,1)} %broadcast_select_fusion.1), calls=%async_computation | async-start | bytes 4194304 | tf_op jit(solution)/shard_map/all_to_all | solution.py:118
  205.7 4.7 copy-start.6
  216.1 10.7 %copy-start.18 = (s32[4,16]{1,0:T(4,128)S(1)}, s32[4,16]{1,0:T(4,128)}, u32[]{:S(2)}) copy-start(s32[4,16]{1,0:T(4,128)} %param.14) | copy-start | bytes 772
  216.1 10.8 %copy-start.10 = (bf16[512,256]{1,0:T(8,128)(2,1)S(1)}, bf16[512,256]{1,0:T(8,128)(2,1)}, u32[]{:S(2)}) copy-start(bf16[512,256]{1,0:T(8,128)(2,1)} %param.19) | copy-start | bytes 786436
  216.1 196.4 %all-to-all-start.1 = ((bf16[64,512,128]{2,1,0:T(8,128)(2,1)}), bf16[64,512,128]{2,1,0:T(8,128)(2,1)}, u32[]{:S(2)}, u32[]{:S(2)}) async-start(bf16[64,512,128]{2,1,0:T(8,128)(2,1)} %stack.2), calls=%async_computation.1 | async-start | bytes 16777216 | tf_op jit(solution)/shard_map/all_to_all | solution.py:14
  412.4 78.9 %all-to-all-start.2 = ((s32[64,1,1]{2,1,0:T(1,128)}), s32[64,1,1]{2,1,0:T(1,128)S(1)}, u32[]{:S(2)}, u32[]{:S(2)}) async-start(s32[64,1,1]{2,1,0:T(1,128)} %copy.91), calls=%async_computation.2 | async-start | bytes 65536 | tf_op jit(solution)/shard_map/all_to_all | solution.py:144
  426.2 1.2 copy-start.4
  426.2 1.3 copy-start.11
  428.4 1.3 copy-start.5
  429.7 1.2 copy-start.2
  436.4 1.2 copy-start.4
  436.4 1.3 copy-start.11
  438.7 1.3 copy-start.5
  446.7 1.2 copy-start.4
  446.7 1.3 copy-start.11
  448.9 1.3 copy-start.5
  456.9 1.2 copy-start.4
  457.0 1.3 copy-start.11
  459.2 1.3 copy-start.5
  491.4 12.5 %copy-start.13 = (bf16[4,128,1,4,64]{1,4,3,2,0:T(8,128)(2,1)S(1)}, bf16[4,128,1,4,64]{1,4,3,2,0:T(8,128)(2,1)}, u32[]{:S(2)}) copy-start(bf16[4,128,1,4,64]{1,4,3,2,0:T(8,128)(2,1)} %get-tuple-element.50) | copy-start | bytes 786436
  491.4 62.0 %all-to-all-start.3 = ((bf16[64,1,128,128]{3,2,1,0:T(8,128)(2,1)}), bf16[64,1,128,128]{3,2,1,0:T(8,128)(2,1)}, u32[]{:S(2)}, u32[]{:S(2)}) async-start(bf16[64,1,128,128]{3,2,1,0:T(8,128)(2,1)} %bitcast.379), calls=%async_computation.3 | async-start | bytes 4194304 | tf_op jit(solution)/shard_map/all_to_all | solution.py:185
  557.4 8.8 %copy-start.7 = (bf16[1024,2,64]{0,2,1:T(8,128)(2,1)S(1)}, bf16[1024,2,64]{0,2,1:T(8,128)(2,1)}, u32[]{:S(2)}) copy-start(bf16[1024,2,64]{0,2,1:T(8,128)(2,1)} %param.18) | copy-start | bytes 786436
  618.3 8.3 %copy-start.19 = (s32[512,1]{0,1:T(1,128)S(1)}, s32[512,1]{0,1:T(1,128)}, u32[]{:S(2)}) copy-start(s32[512,1]{0,1:T(1,128)} %get-tuple-element.387) | copy-start | bytes 6148
  618.3 59.4 %all-to-all-start.4 = ((bf16[64,16,1024]{2,1,0:T(8,128)(2,1)}), bf16[64,16,1024]{2,1,0:T(8,128)(2,1)}, u32[]{:S(2)}, u32[]{:S(2)}) async-start(bf16[64,16,1024]{2,1,0:T(8,128)(2,1)} %broadcast_select_fusion), calls=%async_computation.4 | async-start | bytes 4194304 | tf_op jit(solution)/shard_map/all_to_all | solution.py:202
  626.6 97.3 %reduce-scatter.2.cloned.1.call-start = ((), (), s32[]{:S(2)}) async-start(), calls=%async_computation.7 | async-start | bytes 2621440 | tf_op jit(solution)/shard_map/reduce_scatter | solution.py:213
  677.7 4.6 copy-start.15
  685.1 5.3 copy-start.17
  (10 other events, 11.0 us)
Sparse Core Ops, SparseCore 0:
  28.3 67.4 all-reduce.2
  695.8 28.0 reduce-scatter.1
